TPU v7x, 256 devices: a whole 4x4x8 slice. The times are simulated.
256 devices in a mesh: ctx: 64 (over z, x, core), fsdp: 4 (over y).
Axes of the slice: x: 4, y: 4, z: 8, core: 2. Of those that a mesh axis runs over, the one named last changes fastest.
Arguments:
- queries: bfloat16 [8192, 2048], P('ctx', 'fsdp'), may hold values from -120 to 120
- keys: bfloat16 [8192, 256], P('ctx'), may hold values from -5 to 5
- values: bfloat16 [8192, 256], P('ctx'), may hold values from -5 to 5
- out_grad: bfloat16 [8192, 2048], P('ctx', 'fsdp'), may hold values from -5 to 5
- hidden: bfloat16 [8192, 8192], P('ctx', 'fsdp'), may hold values from -40 to 40
- key_weight: bfloat16 [8192, 256], P('fsdp'), may hold values from -10 to 10
- value_weight: bfloat16 [8192, 256], P('fsdp'), may hold values from -10 to 10
- stretch_owner: int32 [64], replicated, may hold values from 0 to 63, as said below
- positions: int32 [8192], P('ctx'), may hold values from 0 to 4095, as said below
Outputs:
- query_grad: bfloat16 [8192, 2048], P('ctx', 'fsdp')
- key_weight_grad: float32 [8192, 256], P('fsdp')
- value_weight_grad: float32 [8192, 256], P('fsdp')
Inputs may be any that keep to these rules, and one draw needn't show every extreme that they name: A permutation; index b of ctx holds sequence stretch stretch_owner[b] in its first 64 rows and stretch 2 * 64 - 1 - stretch_owner[b] in the others. `positions`: documents are contiguous in sequence order; a row's position counts from its document's first token, and the sequence's first token has position 0.
All inputs are finite; a program needn't handle non-finite values.
Results may differ from a plain program's by a relative error of at most 0.015.
Values may be sent and summed in bfloat16 or wider, within the bound.
A program may use at most 64 MiB of HBM per device.

v0:
```python
import math
import jax
import jax.numpy as jnp
from jax import lax
from jax.sharding import PartitionSpec as P

DH = 128
HPG = 8
KVG = 2
CLIP_RATE = 0.02
EPSILON = 1e-06
NEGATIVE = -1e30


def rows_by_head(block, heads, width):
    count = block.shape[0]
    return block.reshape(count, heads, width).transpose(1, 0, 2).reshape(heads * count, width)


def local(
    queries, keys, values, out_grad, hidden, key_weight, value_weight, stretch_owner, positions
):
    tok_dev = queries.shape[0]
    heads = queries.shape[1] // DH
    ctx_count = lax.axis_size("ctx")
    total = tok_dev * ctx_count
    half = tok_dev // 2
    ctx_index = lax.axis_index("ctx")
    group = lax.axis_index("fsdp") * heads // HPG
    scale = 1.0 / math.sqrt(DH)
    block = min(512, total)
    blocks = total // block
    query_count = heads * tok_dev
    own_keys = lax.dynamic_slice_in_dim(keys, group * DH, DH, 1)
    own_values = lax.dynamic_slice_in_dim(values, group * DH, DH, 1)
    all_keys, all_values = (
        lax.all_gather(own_keys, "ctx", axis=0, tiled=True),
        lax.all_gather(own_values, "ctx", axis=0, tiled=True),
    )
    offsets = jnp.arange(half, dtype=jnp.int32)
    stretches = jnp.stack([stretch_owner, 2 * ctx_count - 1 - stretch_owner], axis=1)
    key_place = (stretches[:, :, None] * half + offsets[None, None, :]).reshape(total)
    mine = lax.dynamic_slice_in_dim(stretches, ctx_index, 1, 0)[0]
    local_place = (mine[:, None] * half + offsets[None, :]).reshape(tok_dev)
    query_place = jnp.tile(local_place, heads)
    query_floor = jnp.tile(local_place - positions, heads)
    query_rows = rows_by_head(queries, heads, DH)
    grad_rows = rows_by_head(out_grad, heads, DH)
    contract_last = (((1,), (1,)), ((), ()))
    contract_first = (((0,), (0,)), ((), ()))

    def scores_at(start, width):
        key_block = lax.dynamic_slice_in_dim(all_keys, start, width, 0)
        place = lax.dynamic_slice_in_dim(key_place, start, width, 0)
        raw = (
            lax.dot_general(
                query_rows, key_block, contract_last, preferred_element_type=jnp.float32
            )
            * scale
        )
        seen = (place[None, :] <= query_place[:, None]) & (place[None, :] >= query_floor[:, None])
        return (jnp.where(seen, raw, NEGATIVE), seen, key_block)

    def stats_step(step, carry):
        top, mass = carry
        masked, seen, key_block = scores_at(step * block, block)
        new_top = jnp.maximum(top, jnp.max(masked, axis=1))
        weights = jnp.where(seen, jnp.exp(masked - new_top[:, None]), 0.0)
        mass = mass * jnp.exp(top - new_top) + jnp.sum(weights, axis=1)
        return (new_top, mass)

    start_top = jnp.full((query_count,), NEGATIVE, jnp.float32)
    start_mass = jnp.zeros((query_count,), jnp.float32)
    top, mass = lax.fori_loop(0, blocks, stats_step, (start_top, start_mass))
    lse = top + jnp.log(mass)

    def probs_at(start, width):
        masked, seen, key_block = scores_at(start, width)
        probs = jnp.where(seen, jnp.exp(masked - lse[:, None]), 0.0)
        value_block = lax.dynamic_slice_in_dim(all_values, start, width, 0)
        dprobs = lax.dot_general(
            grad_rows, value_block, contract_last, preferred_element_type=jnp.float32
        )
        return (probs, dprobs, key_block)

    def delta_step(step, acc):
        probs, dprobs, key_block = probs_at(step * block, block)
        return acc + jnp.sum(probs * dprobs, axis=1)

    delta = lax.fori_loop(0, blocks, delta_step, jnp.zeros((query_count,), jnp.float32))

    def slopes_at(start, width):
        probs, dprobs, key_block = probs_at(start, width)
        slopes = (probs * (dprobs - delta[:, None]) * scale).astype(jnp.bfloat16)
        return (probs.astype(jnp.bfloat16), slopes, key_block)

    def key_terms(probs_b, slopes):
        key_part = lax.dot_general(
            slopes, query_rows, contract_first, preferred_element_type=jnp.float32
        )
        value_part = lax.dot_general(
            probs_b, grad_rows, contract_first, preferred_element_type=jnp.float32
        )
        return jnp.concatenate([key_part, value_part], axis=1)

    start_query = jnp.zeros((query_count, DH), jnp.float32)

    def full_step(step, carry):
        query_acc, terms = carry
        start = step * block
        probs_b, slopes, key_block = slopes_at(start, block)
        query_acc = query_acc + jnp.dot(slopes, key_block, preferred_element_type=jnp.float32)
        terms = lax.dynamic_update_slice_in_dim(terms, key_terms(probs_b, slopes), start, 0)
        return (query_acc, terms)

    start_terms = jnp.zeros((total, 2 * DH), jnp.float32)
    query_acc, terms = lax.fori_loop(0, blocks, full_step, (start_query, start_terms))
    own_grads = lax.psum_scatter(terms, "ctx", scatter_dimension=0, tiled=True)
    query_grad = (
        query_acc.reshape(heads, tok_dev, DH)
        .transpose(1, 0, 2)
        .reshape(tok_dev, heads * DH)
        .astype(jnp.bfloat16)
    )
    members = lax.all_gather(own_grads.astype(jnp.bfloat16), "fsdp", axis=0, tiled=True).astype(
        own_grads.dtype
    )
    per_group = members.reshape(KVG, -1, tok_dev, 2 * DH).sum(axis=1)
    key_grads = (
        per_group[:, :, :DH].transpose(1, 0, 2).reshape(tok_dev, KVG * DH).astype(jnp.bfloat16)
    )
    value_grads = (
        per_group[:, :, DH:].transpose(1, 0, 2).reshape(tok_dev, KVG * DH).astype(jnp.bfloat16)
    )
    both_grads = jnp.concatenate([key_grads, value_grads], axis=1)
    columns = KVG * DH
    raw = lax.psum(
        lax.dot_general(hidden, both_grads, contract_first, preferred_element_type=jnp.float32),
        "ctx",
    )
    key_f = key_weight.astype(jnp.float32)
    value_f = value_weight.astype(jnp.float32)
    grad_sq, key_sq, value_sq = lax.psum(
        (
            jnp.sum(raw * raw, axis=0),
            jnp.sum(key_f * key_f, axis=0),
            jnp.sum(value_f * value_f, axis=0),
        ),
        "fsdp",
    )
    weight_norm = jnp.sqrt(jnp.concatenate([key_sq, value_sq]) + EPSILON)
    grad_norm = jnp.sqrt(grad_sq + EPSILON)
    clipped = raw * jnp.minimum(1.0, CLIP_RATE * total * weight_norm / grad_norm)[None, :]
    return (query_grad, clipped[:, :columns], clipped[:, columns:])


def solution(mesh):
    return jax.shard_map(
        local,
        mesh=mesh,
        in_specs=(
            P("ctx", "fsdp"),
            P("ctx", None),
            P("ctx", None),
            P("ctx", "fsdp"),
            P("ctx", "fsdp"),
            P("fsdp", None),
            P("fsdp", None),
            P(),
            P("ctx"),
        ),
        out_specs=(P("ctx", "fsdp"), P("fsdp", None), P("fsdp", None)),
        check_vma=False,
    )
```

profile of v0, /device:TPU:2, one launch (start us, length us, event | category | flops | bytes accessed | tf_op | source)
XLA Modules:
  0.0 693.1 jit_solution(3216926837924583909)
XLA Ops:
  7.2 1.4 constant_dynamic-slice_fusion.1
  8.7 1.4 constant_dynamic-slice_fusion
  14.8 75.9 %all-gather.3.cloned.1.call-done = bf16[8192,128]{1,0:T(8,128)(2,1)} async-done(((bf16[128,128]{1,0:T(8,128)(2,1)}), bf16[8192,128]{1,0:T(8,128)(2,1)}) %all-gather.3.cloned.1.call-update) | async-done | bytes 2097168 | tf_op jit(solution)/shard_map/all_gather | solution.py:37
  90.7 28.2 %while.46 = (s32[]{:T(128)}, f32[512]{0:T(512)S(1)}, f32[512]{0:T(512)S(1)}, s32[8192]{0:T(1024)S(1)}, bf16[8192,128]{1,0:T(8,128)(2,1)}, /*index=5*/bf16[512,12...) while((s32[]{:T(128)}, f32[512]{0:T(512)S(1)}, ...), condition=%wide.region_3.4_spmd.clone, body=%wide.region_0.3_spmd.clone.sunk | while | flops 70257160 | bytes 2407614 | solution.py:74
  118.9 50.1 %all-gather.5.cloned.1.call-done = bf16[8192,128]{1,0:T(8,128)(2,1)} async-done(((bf16[128,128]{1,0:T(8,128)(2,1)}), bf16[8192,128]{1,0:T(8,128)(2,1)}) %all-gather.5.cloned.1.call-update) | async-done | bytes 2097168 | tf_op jit(solution)/shard_map/all_gather | solution.py:38
  169.0 43.4 %while.47 = (s32[]{:T(128)}, f32[512]{0:T(512)S(1)}, s32[8192]{0:T(1024)S(1)}, bf16[8192,128]{1,0:T(8,128)(2,1)}, bf16[512,128]{1,0:T(8,128)(2,1)S(1)}, /*index=...) while((s32[]{:T(128)}, f32[512]{0:T(512)S(1)}, ...), condition=%wide.region_6.7_spmd.clone, body=%wide.region_4.6_spmd.clone.sunk | while | flops 136577536 | bytes 2647249 | solution.py:90
  169.1 1.4 fusion.98
  171.8 1.4 fusion.98
  174.5 1.4 fusion.98
  177.2 1.4 fusion.98
  180.0 1.4 fusion.98
  182.7 1.4 fusion.98
  185.4 1.4 fusion.98
  188.1 1.4 fusion.98
  190.8 1.4 fusion.98
  193.5 1.4 fusion.98
  196.3 1.4 fusion.98
  199.0 1.4 fusion.98
  201.7 1.4 fusion.98
  204.4 1.4 fusion.98
  207.1 1.4 fusion.98
  209.8 1.4 fusion.98
  212.4 4.2 broadcast_in_dim.81
  216.6 86.9 %while.48 = (s32[]{:T(128)}, f32[512,128]{1,0:T(8,128)S(1)}, f32[8192,256]{0,1:T(8,128)}, s32[8192]{0:T(1024)S(1)}, bf16[8192,128]{1,0:T(8,128)(2,1)}, /*index=5...) while((s32[]{:T(128)}, f32[512,128]{1,0:T(8,128)S(1)}, ...), condition=%wide.region_8.9_spmd.clone, body=%wide.region_7.8_spmd.clone.sunk | while | flops 338952192 | bytes 7752937 | solution.py:117
  216.7 1.4 fusion.110
  222.2 1.4 fusion.110
  227.6 1.4 fusion.110
  233.1 1.4 fusion.110
  238.5 1.4 fusion.110
  243.9 1.4 fusion.110
  249.3 1.4 fusion.110
  260.2 1.4 fusion.110
  265.6 1.4 fusion.110
  271.1 1.4 fusion.110
  276.5 1.4 fusion.110
  281.9 1.4 fusion.110
  287.4 1.4 fusion.110
  292.8 1.3 fusion.110
  303.6 150.1 %reduce-scatter.2.cloned.1.call-done = f32[128,256]{0,1:T(8,128)} async-done(((f32[8192,256]{0,1:T(8,128)}), f32[128,256]{0,1:T(8,128)}) %reduce-scatter.2.cloned.1.call-update) | async-done | bytes 131088 | tf_op jit(solution)/shard_map/reduce_scatter | solution.py:118
  454.7 11.9 %all_gather.11 = bf16[512,256]{0,1:T(8,128)(2,1)S(1)} all-gather(bf16[128,256]{0,1:T(8,128)(2,1)S(1)} %convert_element_type.54), channel_id=1, replica_groups=mesh['ctx'=64,'fsdp'=4] {'fsdp'}, dimensions={0}, use_global_device_ids=true | all-gather | bytes 327680 | tf_op jit(solution)/shard_map/all_gather | solution.py:125
  467.6 2.7 convolution_bitcast_fusion.1
  473.1 191.5 %all-reduce.3.cloned.1.call-done = f32[2048,512]{0,1:T(8,128)} async-done(((f32[2048,512]{0,1:T(8,128)}), f32[2048,512]{0,1:T(8,128)}) %all-reduce.3.cloned.1.call-update) | async-done | bytes 4194320 | tf_op jit(solution)/shard_map/psum | solution.py:137
  664.6 2.5 multiply_reduce_fusion
  667.1 10.5 %all-reduce = (f32[256]{0:T(256)S(1)}, f32[256]{0:T(256)S(1)}, f32[512]{0:T(512)S(1)}) all-reduce(f32[256]{0:T(256)S(1)} %get-tuple-element.720, f32[256]{0:T(256)S(1)} %get-tuple-element.721, f32[512]{0:T(512)S(1)} %multiply_reduce_fusion), channel_id=1, replica_groups=mesh['ctx'=64,'fsdp'=4] {'fsdp'}, use_global_device_ids=true, to_apply=%region_15.16 | all-reduce | flops 1024 | bytes 8192 | tf_op jit(solution)/shard_map/psum | solution.py:143
  677.6 2.5 broadcast_multiply_fusion
  680.2 1.7 fusion.54
  681.9 2.9 copy.33
  684.8 1.8 copy.34
  (331 shorter events, 125.1 us)
Async XLA Ops:
  7.2 460.4 %copy-start = (bf16[128,2048]{1,0:T(8,128)(2,1)S(1)}, bf16[128,2048]{1,0:T(8,128)(2,1)}, u32[]{:S(2)}) copy-start(bf16[128,2048]{1,0:T(8,128)(2,1)} %param.19) | copy-start | bytes 1572868
  7.2 83.5 %all-gather.3.cloned.1.call-start = ((), (), s32[]{:S(2)}) async-start(), calls=%async_computation.1 | async-start | bytes 2129920 | tf_op jit(solution)/shard_map/all_gather | solution.py:37
  8.7 160.3 %all-gather.5.cloned.1.call-start = ((), (), s32[]{:S(2)}) async-start(), calls=%async_computation.2 | async-start | bytes 2129920 | tf_op jit(solution)/shard_map/all_gather | solution.py:38
  10.1 443.6 %reduce-scatter.2.cloned.1.call-start = ((), (), s32[]{:S(2)}) async-start(), calls=%async_computation.3 | async-start | bytes 8519680 | tf_op jit(solution)/shard_map/reduce_scatter | solution.py:118
  303.6 361.0 %all-reduce.3.cloned.1.call-start = ((), (), s32[]{:S(2)}) async-start(), calls=%async_computation.4 | async-start | bytes 8388608 | tf_op jit(solution)/shard_map/psum | solution.py:137
  470.3 1.2 copy-start.1
  470.3 1.5 copy-start.2
Sparse Core Ops, SparseCore 0:
  11.3 79.3 all-gather.2
  94.0 74.9 all-gather.4
  303.7 150.0 reduce-scatter.1
  470.4 194.1 all-reduce.2
where the time goes:
time: 695 us; the launch traced here: 693 us
  waiting for transfers between devices  468 us (67%)
  matrix products  136 us (20%)
  other arithmetic  29 us (4%)
  blocking collectives  22.4 us (3%)
  local copies, waits for them, and re-layouts  21.9 us (3%)
  between operations  13.9 us (2%)
    psum x1, waiting for transfers between devices, local(): lax.psum(lax.dot_general(hidden, both_grads, contract_first, preferred_el...  192 us
    reduce_scatter x1, waiting for transfers between devices, local(): own_grads = lax.psum_scatter(terms, 'ctx', scatter_dimension=0, tiled=True)  150 us
    all_gather x1, waiting for transfers between devices, local(): lax.all_gather(own_keys, 'ctx', axis=0, tiled=True)  75.9 us
    dot_general x48, matrix products, scores_at(): lax.dot_general(query_rows, key_block, contract_last, preferred_element_t...  63.8 us
    all_gather x1, waiting for transfers between devices, local(): lax.all_gather(own_values, 'ctx', axis=0, tiled=True)  50.1 us
    dot_general x32, matrix products, probs_at(): lax.dot_general(grad_rows, value_block, contract_last, preferred_element_...  38.8 us
    dot_general x16, matrix products, full_step(): jnp.dot(slopes, key_block, preferred_element_type=jnp.float32)  20.5 us
  transfers between devices with their start and end apart: 4, of which 4 were waited for; matrix products, arithmetic and copies ran while one was open for 5% of the time, Pallas kernels for 0%

commit v1 on v0

--- a/solution.py
+++ b/solution.py
@@ -35,7 +35,9 @@
     own_values = lax.dynamic_slice_in_dim(values, group * DH, DH, 1)
     all_keys, all_values = (
         lax.all_gather(own_keys, "ctx", axis=0, tiled=True),
-        lax.all_gather(own_values, "ctx", axis=0, tiled=True),
+        jnp.concatenate(
+            lax.all_to_all(jnp.stack([own_values] * lax.axis_size("ctx")), "ctx", 0, 0), axis=0
+        ),
     )
     offsets = jnp.arange(half, dtype=jnp.int32)
     stretches = jnp.stack([stretch_owner, 2 * ctx_count - 1 - stretch_owner], axis=1)

time: 695 us -> 647 us (0.931)
  waiting for transfers between devices: 468 us -> 410 us
  starting transfers between devices: 0.16 us -> 12.5 us
    all_gather x1 -> x0, waiting for transfers between devices: 50.1 us -> none  [local(): lax.all_gather(own_values, 'ctx', axis=0, tiled=True)]
    all_to_all x0 -> x1, starting transfers between devices: none -> 12.3 us  [local(): lax.all_to_all(jnp.stack([own_values] * lax.axis_size('ctx')), 'ctx', 0, 0)]
    all_gather x1, waiting for transfers between devices: 75.9 us -> 67.9 us  [local(): lax.all_gather(own_keys, 'ctx', axis=0, tiled=True)]
  transfers between devices with their start and end apart: 4 -> 4, of which waited for: 4 -> 3; matrix products, arithmetic and copies ran while one was open for 5% -> 5% of each run, Pallas kernels for 0% -> 0%
where the time goes in v1:
time: 647 us; the launch traced here: 645 us
  waiting for transfers between devices  410 us (63%)
  matrix products  136 us (21%)
  other arithmetic  27 us (4%)
  blocking collectives  22.4 us (3%)
  local copies, waits for them, and re-layouts  21.3 us (3%)
  between operations  14 us (2%)
  starting transfers between devices  12.5 us (2%)
    psum x1, waiting for transfers between devices, local(): lax.psum(lax.dot_general(hidden, both_grads, contract_first, preferred_el...  192 us
    reduce_scatter x1, waiting for transfers between devices, local(): own_grads = lax.psum_scatter(terms, 'ctx', scatter_dimension=0, tiled=True)  150 us
    all_gather x1, waiting for transfers between devices, local(): lax.all_gather(own_keys, 'ctx', axis=0, tiled=True)  67.9 us
    dot_general x48, matrix products, scores_at(): lax.dot_general(query_rows, key_block, contract_last, preferred_element_t...  63.8 us
    dot_general x32, matrix products, probs_at(): lax.dot_general(grad_rows, value_block, contract_last, preferred_element_...  38.8 us
    dot_general x16, matrix products, full_step(): jnp.dot(slopes, key_block, preferred_element_type=jnp.float32)  20.6 us
    dynamic_update_slice x16, other arithmetic, full_step(): lax.dynamic_update_slice_in_dim(terms, key_terms(probs_b, slopes), start, 0)  13.7 us
  transfers between devices with their start and end apart: 4, of which 3 were waited for; matrix products, arithmetic and copies ran while one was open for 5% of the time, Pallas kernels for 0%

profile of v1, /device:TPU:2, one launch (start us, length us, event | category | flops | bytes accessed | tf_op | source)
XLA Modules:
  0.0 644.8 jit_solution(1977716977901615153)
XLA Ops:
  7.2 1.4 constant_dynamic-slice_fusion.1
  9.5 1.8 stack.11
  11.3 12.3 %all-to-all-start = ((bf16[64,128,128]{2,1,0:T(8,128)(2,1)}), bf16[64,128,128]{2,1,0:T(8,128)(2,1)}, u32[]{:S(2)}, u32[]{:S(2)}) async-start(bf16[64,128,128]{2,1,0:T(8,128)(2,1)} %stack.11), calls=%async_computation | async-start | bytes 4194304 | tf_op jit(solution)/shard_map/all_to_all | solution.py:39
  24.5 67.9 %all-gather.2.cloned.1.call-done = bf16[8192,128]{1,0:T(8,128)(2,1)} async-done(((bf16[128,128]{1,0:T(8,128)(2,1)}), bf16[8192,128]{1,0:T(8,128)(2,1)}) %all-gather.2.cloned.1.call-update) | async-done | bytes 2097168 | tf_op jit(solution)/shard_map/all_gather | solution.py:37
  92.5 28.2 %while.46 = (s32[]{:T(128)}, f32[512]{0:T(512)S(1)}, f32[512]{0:T(512)S(1)}, s32[8192]{0:T(1024)S(1)}, bf16[8192,128]{1,0:T(8,128)(2,1)}, /*index=5*/bf16[512,12...) while((s32[]{:T(128)}, f32[512]{0:T(512)S(1)}, ...), condition=%wide.region_3.4_spmd.clone, body=%wide.region_0.3_spmd.clone.sunk | while | flops 70257160 | bytes 2407614 | solution.py:76
  120.7 43.4 %while.47 = (s32[]{:T(128)}, f32[512]{0:T(512)S(1)}, s32[8192]{0:T(1024)S(1)}, bf16[8192,128]{1,0:T(8,128)(2,1)}, bf16[512,128]{1,0:T(8,128)(2,1)S(1)}, /*index=...) while((s32[]{:T(128)}, f32[512]{0:T(512)S(1)}, ...), condition=%wide.region_6.7_spmd.clone, body=%wide.region_4.6_spmd.clone.sunk | while | flops 136577536 | bytes 2647249 | solution.py:92
  123.5 1.4 fusion.98
  126.2 1.4 fusion.98
  128.9 1.4 fusion.98
  131.6 1.4 fusion.98
  134.3 1.4 fusion.98
  137.1 1.4 fusion.98
  139.8 1.4 fusion.98
  142.5 1.4 fusion.98
  145.2 1.4 fusion.98
  147.9 1.4 fusion.98
  150.6 1.4 fusion.98
  153.3 1.4 fusion.98
  156.0 1.4 fusion.98
  158.8 1.4 fusion.98
  161.5 1.4 fusion.98
  164.1 4.2 broadcast_in_dim.81
  168.3 87.0 %while.48 = (s32[]{:T(128)}, f32[512,128]{1,0:T(8,128)S(1)}, f32[8192,256]{0,1:T(8,128)}, s32[8192]{0:T(1024)S(1)}, bf16[8192,128]{1,0:T(8,128)(2,1)}, /*index=5...) while((s32[]{:T(128)}, f32[512,128]{1,0:T(8,128)S(1)}, ...), condition=%wide.region_8.9_spmd.clone, body=%wide.region_7.8_spmd.clone.sunk | while | flops 338952192 | bytes 7752937 | solution.py:119
  168.3 1.4 fusion.110
  173.8 1.4 fusion.110
  179.3 1.4 fusion.110
  184.7 1.4 fusion.110
  190.2 1.4 fusion.110
  195.6 1.4 fusion.110
  201.0 1.4 fusion.110
  206.5 1.4 fusion.110
  211.9 1.4 fusion.110
  217.3 1.4 fusion.110
  222.8 1.4 fusion.110
  228.2 1.4 fusion.110
  233.7 1.4 fusion.110
  244.5 1.4 fusion.110
  249.9 1.4 fusion.110
  255.4 150.1 %reduce-scatter.2.cloned.1.call-done = f32[128,256]{0,1:T(8,128)} async-done(((f32[8192,256]{0,1:T(8,128)}), f32[128,256]{0,1:T(8,128)}) %reduce-scatter.2.cloned.1.call-update) | async-done | bytes 131088 | tf_op jit(solution)/shard_map/reduce_scatter | solution.py:120
  406.4 11.9 %all_gather.7 = bf16[512,256]{0,1:T(8,128)(2,1)S(1)} all-gather(bf16[128,256]{0,1:T(8,128)(2,1)S(1)} %convert_element_type.54), channel_id=1, replica_groups=mesh['ctx'=64,'fsdp'=4] {'fsdp'}, dimensions={0}, use_global_device_ids=true | all-gather | bytes 327680 | tf_op jit(solution)/shard_map/all_gather | solution.py:127
  419.3 2.7 convolution_bitcast_fusion.1
  424.8 191.5 %all-reduce.3.cloned.1.call-done = f32[2048,512]{0,1:T(8,128)} async-done(((f32[2048,512]{0,1:T(8,128)}), f32[2048,512]{0,1:T(8,128)}) %all-reduce.3.cloned.1.call-update) | async-done | bytes 4194320 | tf_op jit(solution)/shard_map/psum | solution.py:139
  616.3 2.5 multiply_reduce_fusion
  618.8 10.5 %all-reduce = (f32[256]{0:T(256)S(1)}, f32[256]{0:T(256)S(1)}, f32[512]{0:T(512)S(1)}) all-reduce(f32[256]{0:T(256)S(1)} %get-tuple-element.720, f32[256]{0:T(256)S(1)} %get-tuple-element.721, f32[512]{0:T(512)S(1)} %multiply_reduce_fusion), channel_id=1, replica_groups=mesh['ctx'=64,'fsdp'=4] {'fsdp'}, use_global_device_ids=true, to_apply=%region_15.16 | all-reduce | flops 1024 | bytes 8192 | tf_op jit(solution)/shard_map/psum | solution.py:145
  629.3 2.5 broadcast_multiply_fusion
  631.9 1.7 fusion.54
  633.6 2.9 copy.33
  636.4 1.8 copy.34
  (339 shorter events, 122.1 us)
Async XLA Ops:
  7.2 412.1 %copy-start = (bf16[128,2048]{1,0:T(8,128)(2,1)S(1)}, bf16[128,2048]{1,0:T(8,128)(2,1)}, u32[]{:S(2)}) copy-start(bf16[128,2048]{1,0:T(8,128)(2,1)} %param.19) | copy-start | bytes 1572868
  7.2 85.3 %all-gather.2.cloned.1.call-start = ((), (), s32[]{:S(2)}) async-start(), calls=%async_computation.2 | async-start | bytes 2129920 | tf_op jit(solution)/shard_map/all_gather | solution.py:37
  11.3 12.5 %copy-start.5 = (s32[64]{0:T(128)S(1)}, s32[64]{0:T(128)}, u32[]{:S(2)}) copy-start(s32[64]{0:T(128)} %param.22) | copy-start | bytes 772
  11.3 13.2 %copy-start.6 = (s32[128]{0:T(128)S(1)}, s32[128]{0:T(128)}, u32[]{:S(2)}) copy-start(s32[128]{0:T(128)} %param.23) | copy-start | bytes 1540
  11.3 13.2 %copy-start.3 = (bf16[128,512]{1,0:T(8,128)(2,1)S(1)}, bf16[128,512]{1,0:T(8,128)(2,1)}, u32[]{:S(2)}) copy-start(bf16[128,512]{1,0:T(8,128)(2,1)} %param.15) | copy-start | bytes 393220
  11.3 13.2 %copy-start.4 = (bf16[128,512]{1,0:T(8,128)(2,1)S(1)}, bf16[128,512]{1,0:T(8,128)(2,1)}, u32[]{:S(2)}) copy-start(bf16[128,512]{1,0:T(8,128)(2,1)} %param.18) | copy-start | bytes 393220
  11.3 109.4 %all-to-all-start = ((bf16[64,128,128]{2,1,0:T(8,128)(2,1)}), bf16[64,128,128]{2,1,0:T(8,128)(2,1)}, u32[]{:S(2)}, u32[]{:S(2)}) async-start(bf16[64,128,128]{2,1,0:T(8,128)(2,1)} %stack.11), calls=%async_computation | async-start | bytes 4194304 | tf_op jit(solution)/shard_map/all_to_all | solution.py:39
  23.7 381.8 %reduce-scatter.2.cloned.1.call-start = ((), (), s32[]{:S(2)}) async-start(), calls=%async_computation.3 | async-start | bytes 8519680 | tf_op jit(solution)/shard_map/reduce_scatter | solution.py:120
  255.3 361.0 %all-reduce.3.cloned.1.call-start = ((), (), s32[]{:S(2)}) async-start(), calls=%async_computation.4 | async-start | bytes 8388608 | tf_op jit(solution)/shard_map/psum | solution.py:139
  422.0 1.2 copy-start.1
  422.0 1.5 copy-start.2
Sparse Core Ops, SparseCore 0:
  11.3 81.0 all-gather.1
  255.5 149.9 reduce-scatter.1
  422.1 194.1 all-reduce.2
